TPU v7x, 128 devices: a whole 4x4x4 slice. The times are simulated.
128 devices in a mesh: req: 32 (over y, x, core), head: 4 (over z).
Axes of the slice: x: 4, y: 4, z: 4, core: 2. Of those that a mesh axis runs over, the one named last changes fastest.
Arguments:
- hidden_in: bfloat16 [1024, 5120], P('req'), may hold values from -60 to 60
- query: bfloat16 [1024, 4096], P('req', 'head'), may hold values from -12 to 12
- incoming_key: bfloat16 [1024, 1024], P('req', 'head'), may hold values from -6 to 6
- incoming_value: bfloat16 [1024, 1024], P('req', 'head'), may hold values from -6 to 6
- private_tail_keys: bfloat16 [1024, 160, 1024], P('req', None, 'head'), may hold values from -6 to 6
- private_tail_values: bfloat16 [1024, 160, 1024], P('req', None, 'head'), may hold values from -6 to 6
- group_prompt_keys: bfloat16 [96, 512, 1024], P('req', None, 'head'), may hold values from -6 to 6
- group_prompt_values: bfloat16 [96, 512, 1024], P('req', None, 'head'), may hold values from -6 to 6
- group_id: int32 [1024], P('req'), may hold values from 0 to 95, as said below
- prompt_len: int32 [96], P('req'), may hold values from 128 to 512, as said below
- tail_len: int32 [1024], P('req'), may hold values from 0 to 159, as said below
- out_proj: bfloat16 [4096, 5120], P('head'), may hold values from -0.5 to 0.5
- norm_gain: float32 [5120], replicated, may hold values from 0.1 to 1.9
- gate_proj: bfloat16 [5120, 32768], P(None, ('req', 'head')), may hold values from -0.078125 to 0.078125
- up_proj: bfloat16 [5120, 32768], P(None, ('req', 'head')), may hold values from -0.078125 to 0.078125
- down_proj: bfloat16 [32768, 5120], P('req', 'head'), may hold values from -0.03125 to 0.03125
Outputs:
- layer_out: bfloat16 [1024, 5120], P(('req', 'head'))
Inputs may be any that keep to these rules, and one draw needn't show every extreme that they name: `group_id`: the prompt cache of group g is held by index g // 3 of req. Among the 32 requests of one index of req, at most 2 belong to groups held by any one index of req; in every draw one index of req holds the groups of exactly 2 requests of every index of req. `prompt_len`: some group's prompt fills all 512 positions. Request r's earlier private tokens are in slots 0 to tail_len[r] - 1; some request has 159 of them.
All inputs are finite; a program needn't handle non-finite values.
Results may differ from a plain program's by a relative error of at most 0.007.
Values may be sent and summed in bfloat16 or wider, within the bound.
No kernel may reach another device: no remote copies, remote signals or barrier semaphores. Data moves between devices by JAX's collectives and lax.ppermute only.
A program may use at most 128 MiB of HBM per device.

v0:
```python
import jax
import jax.numpy as jnp
from jax import lax
from jax.sharding import PartitionSpec as P

QUERY_HEADS = 32
KEY_VALUE_HEADS = 8
HEAD_WIDTH = 128
MASKED_SCORE = -1e30


def shards(
    hidden_in,
    query,
    incoming_key,
    incoming_value,
    private_tail_keys,
    private_tail_values,
    group_prompt_keys,
    group_prompt_values,
    group_id,
    prompt_len,
    tail_len,
    out_proj,
    norm_gain,
    gate_proj,
    up_proj,
    down_proj,
):
    n_req = lax.axis_size("req")
    n_head = lax.axis_size("head")
    row_count = query.shape[0]
    kv_local = incoming_key.shape[1] // HEAD_WIDTH
    each_key_value = QUERY_HEADS // KEY_VALUE_HEADS
    group_count = prompt_len.shape[0]
    prompt_size = group_prompt_keys.shape[1]
    tail_size = private_tail_keys.shape[1]
    slot_cap = 2 * row_count // n_req
    slot_total = n_req * slot_cap
    scale_of_scores = HEAD_WIDTH ** (-0.5)
    col_width = query.shape[1]
    head_local = kv_local * each_key_value
    holder = group_id // group_count
    local_group = group_id - holder * group_count
    holder_hot = (holder[:, None] == jnp.arange(n_req)[None, :]).astype(jnp.int32)
    before = jnp.cumsum(holder_hot, axis=0) - holder_hot
    order_in = jnp.sum(before * holder_hot, axis=1)
    slot_of = holder * slot_cap + order_in
    placing = slot_of[:, None] == jnp.arange(slot_total)[None, :]
    send_query = (
        jnp.einsum(
            "rs,rc->sc", placing.astype(jnp.bfloat16), query, preferred_element_type=jnp.float32
        )
        .astype(jnp.bfloat16)
        .reshape(n_req, slot_cap, col_width)
    )
    send_group = (
        jnp.sum(placing.astype(jnp.int32) * (local_group[:, None] + 1), axis=0) - 1
    ).reshape(n_req, slot_cap)
    keys_all = group_prompt_keys.reshape(group_count * prompt_size, kv_local, HEAD_WIDTH)
    values_all = group_prompt_values.reshape(group_count * prompt_size, kv_local, HEAD_WIDTH)
    key_group = jnp.arange(group_count * prompt_size) // prompt_size
    key_live = jnp.arange(group_count * prompt_size) % prompt_size < jnp.repeat(
        prompt_len, prompt_size
    )
    recv_query = lax.all_to_all(send_query, "req", split_axis=0, concat_axis=0, tiled=True)
    recv_group = lax.all_to_all(send_group, "req", split_axis=0, concat_axis=0, tiled=True)
    sources, item_count = recv_group.shape
    flat_query = recv_query.reshape(sources * item_count, kv_local, each_key_value, HEAD_WIDTH)
    scores = (
        jnp.einsum("nkrd,pkd->nkrp", flat_query, keys_all, preferred_element_type=jnp.float32)
        * scale_of_scores
    )
    usable = (recv_group.reshape(sources * item_count)[:, None] == key_group[None, :]) & key_live[
        None, :
    ]
    masked = jnp.where(usable[:, None, None, :], scores, MASKED_SCORE)
    largest = jnp.max(masked, axis=-1)
    weights = jnp.exp(masked - largest[..., None])
    totals = jnp.sum(weights, axis=-1)
    mixture = jnp.einsum(
        "nkrp,pkd->nkrd",
        weights.astype(jnp.bfloat16),
        values_all,
        preferred_element_type=jnp.float32,
    )
    back_mix = lax.all_to_all(
        mixture.reshape(sources, item_count, col_width),
        "req",
        split_axis=0,
        concat_axis=0,
        tiled=True,
    )
    back_peak = lax.all_to_all(
        largest.reshape(sources, item_count, head_local),
        "req",
        split_axis=0,
        concat_axis=0,
        tiled=True,
    )
    back_total = lax.all_to_all(
        totals.reshape(sources, item_count, head_local),
        "req",
        split_axis=0,
        concat_axis=0,
        tiled=True,
    )
    shared_mix = jnp.take(back_mix.reshape(slot_total, col_width), slot_of, axis=0).reshape(
        row_count, kv_local, each_key_value, HEAD_WIDTH
    )
    shared_max = jnp.take(back_peak.reshape(slot_total, head_local), slot_of, axis=0).reshape(
        row_count, kv_local, each_key_value
    )
    shared_total = jnp.take(back_total.reshape(slot_total, head_local), slot_of, axis=0).reshape(
        row_count, kv_local, each_key_value
    )
    query_rows = query.reshape(row_count, kv_local, each_key_value, HEAD_WIDTH)
    request_keys = private_tail_keys.reshape(row_count, tail_size, kv_local, HEAD_WIDTH)
    request_values = private_tail_values.reshape(row_count, tail_size, kv_local, HEAD_WIDTH)
    tail_scores = (
        jnp.einsum("bkrd,btkd->bkrt", query_rows, request_keys, preferred_element_type=jnp.float32)
        * scale_of_scores
    )
    current_scores = (
        jnp.einsum(
            "ivxg,ivg->ivx",
            query_rows,
            incoming_key.reshape(row_count, kv_local, HEAD_WIDTH),
            preferred_element_type=jnp.float32,
        )
        * scale_of_scores
    )
    tail_live = (jnp.arange(tail_size)[None, :] < tail_len[:, None])[:, None, None, :]
    tail_masked = jnp.where(tail_live, tail_scores, MASKED_SCORE)
    local_max = jnp.maximum(jnp.max(tail_masked, axis=-1), current_scores)
    tail_exp = jnp.exp(tail_masked - local_max[..., None])
    fresh_exp = jnp.exp(current_scores - local_max)
    local_total = jnp.sum(tail_exp, axis=-1) + fresh_exp
    fresh_weights = lax.optimization_barrier(fresh_exp.astype(jnp.bfloat16)).astype(jnp.float32)
    fresh_vals = incoming_value.reshape(row_count, kv_local, HEAD_WIDTH).astype(jnp.float32)
    local_mix = (
        jnp.einsum(
            "bkrt,btkd->bkrd",
            tail_exp.astype(jnp.bfloat16),
            request_values,
            preferred_element_type=jnp.float32,
        )
        + fresh_weights[..., None] * fresh_vals[:, :, None, :]
    )
    highest = jnp.maximum(shared_max, local_max)
    shared_factor = jnp.exp(shared_max - highest)
    local_factor = jnp.exp(local_max - highest)
    numer = shared_mix * shared_factor[..., None] + local_mix * local_factor[..., None]
    denom = shared_total * shared_factor + local_total * local_factor
    attention = (numer / denom[..., None]).reshape(row_count, col_width).astype(jnp.bfloat16)
    projected = jnp.dot(attention, out_proj, preferred_element_type=jnp.float32)
    sub_rows = row_count // n_head
    head_index = lax.axis_index("head")
    summed = lax.psum(projected, "head")
    residual = (hidden_in.astype(jnp.float32) + summed).astype(jnp.bfloat16)
    resid_f = residual.astype(jnp.float32)
    segment = lax.all_gather(
        (
            resid_f
            * lax.rsqrt(jnp.mean(resid_f * resid_f, axis=-1, keepdims=True) + 1e-05)
            * norm_gain
        ).astype(jnp.bfloat16),
        "req",
        axis=0,
        tiled=True,
    )
    gate_vals = jnp.dot(segment, gate_proj, preferred_element_type=jnp.float32)
    up_vals = jnp.dot(segment, up_proj, preferred_element_type=jnp.float32)
    hidden = (jax.nn.silu(gate_vals) * up_vals).astype(jnp.bfloat16)
    own_rows = lax.dynamic_slice_in_dim(residual, head_index * sub_rows, sub_rows, 0)
    down_rows = lax.all_to_all(down_proj, "head", split_axis=0, concat_axis=1, tiled=True)
    lowered = lax.psum_scatter(
        jnp.dot(hidden, down_rows, preferred_element_type=jnp.float32),
        ("req", "head"),
        scatter_dimension=0,
        tiled=True,
    )
    return (own_rows.astype(jnp.float32) + lowered).astype(jnp.bfloat16)


def solution(mesh):
    return jax.shard_map(
        shards,
        mesh=mesh,
        in_specs=(
            P("req", None),
            P("req", "head"),
            P("req", "head"),
            P("req", "head"),
            P("req", None, "head"),
            P("req", None, "head"),
            P("req", None, "head"),
            P("req", None, "head"),
            P("req"),
            P("req"),
            P("req"),
            P("head", None),
            P(),
            P(None, ("req", "head")),
            P(None, ("req", "head")),
            P("req", "head"),
        ),
        out_specs=P(("req", "head"), None),
        check_vma=False,
    )
```

profile of v0, /device:TPU:0, one launch (start us, length us, event | category | flops | bytes accessed | tf_op | source)
XLA Modules:
  0.0 910.8 jit_solution(5117704881106043649)
XLA Ops:
  9.0 7.4 all-to-all-start
  20.5 3.3 fusion.65
  27.1 2.0 reshape.202
  29.2 7.5 all-to-all-start.1
  38.8 5.7 all-to-all-done.1
  44.5 1.6 reshape.201
  46.1 1.7 fusion.66
  51.0 3.9 all-to-all-start.4
  55.5 2.0 reshape.203
  59.8 2.5 all-to-all-done.4
  62.2 4.9 all-to-all-start.3
  67.2 2.6 fusion.20
  71.5 3.0 all-to-all-done.3
  74.6 4.4 all-to-all-start.2
  82.0 5.8 all-to-all-done.2
  88.9 2.6 fusion.35
  91.6 6.8 fusion.68
  98.6 42.6 %all-reduce.2.cloned.1.call-done = f32[32,5120]{1,0:T(8,128)} async-done(((f32[32,5120]{1,0:T(8,128)}), f32[32,5120]{1,0:T(8,128)}) %all-reduce.2.cloned.1.call-update) | async-done | bytes 655376 | tf_op jit(solution)/shard_map/psum | solution.py:159
  143.4 35.0 %all_to_all.45 = bf16[4,256,1280]{2,1,0:T(8,128)(2,1)} all-to-all(bf16[4,256,1280]{2,1,0:T(8,128)(2,1)} %bitcast.79), channel_id=1, replica_groups=mesh['req'=32,'head'=4] {'head'}, dimensions={0} | all-to-all | bytes 5242880 | tf_op jit(solution)/shard_map/all_to_all | solution.py:176
  178.4 4.4 copy.99
  182.8 19.0 %all-gather.2.cloned.1.call-done = bf16[1024,5120]{1,0:T(8,128)(2,1)} async-done(((bf16[32,5120]{1,0:T(8,128)(2,1)}), bf16[1024,5120]{1,0:T(8,128)(2,1)}) %all-gather.2.cloned.1.call-update) | async-done | bytes 10485776 | tf_op jit(solution)/shard_map/all_gather | solution.py:162
  201.8 8.6 fusion.69
  210.4 18.4 %fusion.70 = f32[1024,5120]{1,0:T(8,128)} fusion(bf16[256,5120]{0,1:T(8,128)(2,1)} %bitcast.75, bf16[1024,5120]{1,0:T(8,128)(2,1)} %all-gather.2.cloned.1.call-done, bf16[5120,256]{1,0:T(8,128)(2,1)S(1)} %copy-done, f32[1024,256]{1,0:T(8,128)} %fusion.69), kind=kOutput, calls=%fused_computation.86 | convolution fusion | flops 5370281984 | bytes 37748736 | tf_op jit(solution)/shard_map/dot_general | solution.py:178
  228.8 673.9 %reduce-scatter.2.cloned.1.call-done = f32[8,5120]{1,0:T(8,128)} async-done(((f32[1024,5120]{1,0:T(8,128)}), f32[8,5120]{1,0:T(8,128)}) %reduce-scatter.2.cloned.1.call-update) | async-done | bytes 163856 | tf_op jit(solution)/shard_map/reduce_scatter | solution.py:177
  (87 shorter events, 27.8 us)
Async XLA Ops:
  6.5 203.8 %copy-start = (bf16[5120,256]{1,0:T(8,128)(2,1)S(1)}, bf16[5120,256]{1,0:T(8,128)(2,1)}, u32[]{:S(2)}) copy-start(bf16[5120,256]{1,0:T(8,128)(2,1)} %param.32) | copy-start | bytes 7864324
  6.5 17.4 %copy-start.8 = (bf16[32,256]{1,0:T(8,128)(2,1)S(1)}, bf16[32,256]{1,0:T(8,128)(2,1)}, u32[]{:S(2)}) copy-start(bf16[32,256]{1,0:T(8,128)(2,1)} %param.20) | copy-start | bytes 49156
  9.0 20.1 %all-to-all-start = ((s32[32,1,2]{2,1,0:T(1,128)}), s32[32,1,2]{2,1,0:T(1,128)S(1)}, u32[]{:S(2)}, u32[]{:S(2)}) async-start(s32[32,1,2]{2,1,0:T(1,128)} %bitcast), calls=%async_computation | async-start | bytes 32768 | tf_op jit(solution)/shard_map/all_to_all | solution.py:67
  23.8 2.6 copy-start.4
  29.2 15.3 %all-to-all-start.1 = ((bf16[32,2,1024]{2,1,0:T(2,128)(2,1)}), bf16[32,2,1024]{2,1,0:T(2,128)(2,1)}, u32[]{:S(2)}, u32[]{:S(2)}) async-start(bf16[32,2,1024]{2,1,0:T(2,128)(2,1)} %reshape.200), calls=%async_computation.1 | async-start | bytes 262144 | tf_op jit(solution)/shard_map/all_to_all | solution.py:66
  47.8 1.7 copy-start.2
  47.8 7.0 copy-start.11
  47.8 7.6 copy-start.6
  47.9 9.7 %copy-start.10 = (bf16[32,2,4]{0,2,1:T(4,128)(2,1)S(1)}, bf16[32,2,4]{0,2,1:T(4,128)(2,1)}, u32[]{:S(2)}) copy-start(bf16[32,2,4]{0,2,1:T(4,128)(2,1)} %get-tuple-element.8) | copy-start | bytes 1540
  47.9 10.4 %copy-start.9 = (bf16[32,256]{1,0:T(8,128)(2,1)S(1)}, bf16[32,256]{1,0:T(8,128)(2,1)}, u32[]{:S(2)}) copy-start(bf16[32,256]{1,0:T(8,128)(2,1)} %param.21) | copy-start | bytes 49156
  51.0 11.3 %all-to-all-start.4 = ((f32[32,2,8]{2,1,0:T(2,128)}), f32[32,2,8]{2,1,0:T(2,128)S(1)}, u32[]{:S(2)}, u32[]{:S(2)}) async-start(f32[32,2,8]{2,1,0:T(2,128)} %reshape.213), calls=%async_computation.4 | async-start | bytes 65536 | tf_op jit(solution)/shard_map/all_to_all | solution.py:101
  62.2 12.3 %all-to-all-start.3 = ((f32[32,2,8]{2,1,0:T(2,128)}), f32[32,2,8]{2,1,0:T(2,128)S(1)}, u32[]{:S(2)}, u32[]{:S(2)}) async-start(f32[32,2,8]{2,1,0:T(2,128)} %reshape.206), calls=%async_computation.3 | async-start | bytes 65536 | tf_op jit(solution)/shard_map/all_to_all | solution.py:94
  69.8 19.1 %copy-start.5 = (f32[32,2,4,160]{3,2,1,0:T(4,128)S(1)}, f32[32,2,4,160]{3,2,1,0:T(4,128)}, u32[]{:S(2)}) copy-start(f32[32,2,4,160]{3,2,1,0:T(4,128)} %copy-done.4) | copy-start | bytes 491524
  74.6 13.3 %all-to-all-start.2 = ((f32[32,2,1024]{2,1,0:T(2,128)}), f32[32,2,1024]{2,1,0:T(2,128)S(1)}, u32[]{:S(2)}, u32[]{:S(2)}) async-start(f32[32,2,1024]{2,1,0:T(2,128)} %reshape.204), calls=%async_computation.2 | async-start | bytes 524288 | tf_op jit(solution)/shard_map/all_to_all | solution.py:87
  78.9 62.2 %all-reduce.2.cloned.1.call-start = ((), (), s32[]{:S(2)}) async-start(), calls=%async_computation.7 | async-start | bytes 1310720 | tf_op jit(solution)/shard_map/psum | solution.py:159
  91.5 49.6 %copy-start.3 = (bf16[32,5120]{1,0:T(8,128)(2,1)S(1)}, bf16[32,5120]{1,0:T(8,128)(2,1)}, u32[]{:S(2)}) copy-start(bf16[32,5120]{1,0:T(8,128)(2,1)} %param.18) | copy-start | bytes 983044
  91.5 50.9 %copy-start.7 = (f32[5120]{0:T(1024)S(1)}, f32[5120]{0:T(1024)}, u32[]{:S(2)}) copy-start(f32[5120]{0:T(1024)} %param.30) | copy-start | bytes 61444
  98.4 103.4 %all-gather.2.cloned.1.call-start = ((), (), s32[]{:S(2)}) async-start(), calls=%async_computation.8 | async-start | bytes 10813440 | tf_op jit(solution)/shard_map/all_gather | solution.py:162
  143.4 759.3 %reduce-scatter.2.cloned.1.call-start = ((), (), s32[]{:S(2)}) async-start(), calls=%async_computation.9 | async-start | bytes 21135360 | tf_op jit(solution)/shard_map/reduce_scatter | solution.py:177
  228.8 675.5 %copy-start.1 = (bf16[5120,256]{1,0:T(8,128)(2,1)S(1)}, bf16[5120,256]{1,0:T(8,128)(2,1)}, u32[]{:S(2)}) copy-start(bf16[5120,256]{1,0:T(8,128)(2,1)} %param.32) | copy-start | bytes 7864324
Sparse Core Ops, SparseCore 0:
  98.5 42.6 all-reduce.1
  143.5 58.2 all-gather.1
  229.0 673.7 reduce-scatter.1
where the time goes:
time: 912 us; the launch traced here: 911 us
  waiting for transfers between devices  753 us (83%)
  matrix products  45.3 us (5%)
  blocking collectives  35 us (4%)
  starting transfers between devices  28.4 us (3%)
  local copies, waits for them, and re-layouts  23.9 us (3%)
  between operations  13.4 us (1%)
  other arithmetic  12.3 us (1%)
    reduce_scatter x1, waiting for transfers between devices, shards(): lax.psum_scatter(jnp.dot(hidden, down_rows, preferred_element_type=jnp.fl...  674 us
    psum x1, waiting for transfers between devices, shards(): summed = lax.psum(projected, 'head')  42.6 us
    all_to_all x1, blocking collectives, shards(): lax.all_to_all(down_proj, 'head', split_axis=0, concat_axis=1, tiled=True)  35 us
    all_gather x1, waiting for transfers between devices, shards(): lax.all_gather((resid_f * lax.rsqrt(jnp.mean(resid_f * resid_f, axis=-1,...  19 us
    dot_general x1, matrix products, shards(): jnp.dot(hidden, down_rows, preferred_element_type=jnp.float32)  18.4 us
  transfers between devices with their start and end apart: 8, of which 7 were waited for; matrix products, arithmetic and copies ran while one was open for 3% of the time, Pallas kernels for 0%

commit v1 on v0

--- a/solution.py
+++ b/solution.py
@@ -156,7 +156,7 @@
     projected = jnp.dot(attention, out_proj, preferred_element_type=jnp.float32)
     sub_rows = row_count // n_head
     head_index = lax.axis_index("head")
-    summed = lax.psum(projected, "head")
+    summed = jnp.sum(lax.all_gather(projected, "head"), axis=0)
     residual = (hidden_in.astype(jnp.float32) + summed).astype(jnp.bfloat16)
     resid_f = residual.astype(jnp.float32)
     segment = lax.all_gather(

time: 912 us -> 906 us (level)
  waiting for transfers between devices: 753 us -> 742 us
    psum x1 -> x0, waiting for transfers between devices: 42.6 us -> none  [shards(): summed = lax.psum(projected, 'head')]
    all_gather x0 -> x1, waiting for transfers between devices: none -> 34.2 us  [shards(): summed = jnp.sum(lax.all_gather(projected, 'head'), axis=0)]
where the time goes in v1:
time: 906 us; the launch traced here: 905 us
  waiting for transfers between devices  742 us (82%)
  matrix products  45.3 us (5%)
  blocking collectives  36.7 us (4%)
  starting transfers between devices  28.4 us (3%)
  local copies, waits for them, and re-layouts  24.7 us (3%)
  other arithmetic  14.2 us (2%)
  between operations  13.4 us (1%)
    reduce_scatter x1, waiting for transfers between devices, shards(): lax.psum_scatter(jnp.dot(hidden, down_rows, preferred_element_type=jnp.fl...  674 us
    all_to_all x1, blocking collectives, shards(): lax.all_to_all(down_proj, 'head', split_axis=0, concat_axis=1, tiled=True)  36.7 us
    all_gather x1, waiting for transfers between devices, shards(): summed = jnp.sum(lax.all_gather(projected, 'head'), axis=0)  34.2 us
    dot_general x1, matrix products, shards(): jnp.dot(hidden, down_rows, preferred_element_type=jnp.float32)  18.4 us
  transfers between devices with their start and end apart: 8, of which 7 were waited for; matrix products, arithmetic and copies ran while one was open for 3% of the time, Pallas kernels for 0%

profile of v1, /device:TPU:0, one launch (start us, length us, event | category | flops | bytes accessed | tf_op | source)
XLA Modules:
  0.0 904.8 jit_solution(4670169929956758651)
XLA Ops:
  9.0 7.4 all-to-all-start
  20.5 3.3 fusion.65
  27.1 2.0 reshape.202
  29.2 7.5 all-to-all-start.1
  38.8 5.7 all-to-all-done.1
  46.1 1.7 fusion.66
  51.0 3.9 all-to-all-start.4
  55.5 2.0 reshape.203
  59.8 2.5 all-to-all-done.4
  62.2 4.9 all-to-all-start.3
  67.2 2.6 fusion.20
  71.5 3.0 all-to-all-done.3
  74.6 4.4 all-to-all-start.2
  82.0 5.8 all-to-all-done.2
  88.9 2.6 fusion.35
  91.5 6.7 fusion.68
  98.5 34.2 %all-gather.6.cloned.1.call-done = f32[128,5120]{1,0:T(8,128)} async-done(((f32[32,5120]{1,0:T(8,128)}), f32[128,5120]{1,0:T(8,128)}) %all-gather.6.cloned.1.call-update) | async-done | bytes 2621456 | tf_op jit(solution)/shard_map/all_gather | solution.py:159
  132.7 2.0 reduce_sum.58
  137.5 36.7 %all_to_all.45 = bf16[4,256,1280]{2,1,0:T(8,128)(2,1)} all-to-all(bf16[4,256,1280]{2,1,0:T(8,128)(2,1)} %bitcast.80), channel_id=1, replica_groups=mesh['req'=32,'head'=4] {'head'}, dimensions={0} | all-to-all | bytes 5242880 | tf_op jit(solution)/shard_map/all_to_all | solution.py:176
  174.2 4.5 copy.99
  178.7 16.5 %all-gather.4.cloned.1.call-done = bf16[1024,5120]{1,0:T(8,128)(2,1)} async-done(((bf16[32,5120]{1,0:T(8,128)(2,1)}), bf16[1024,5120]{1,0:T(8,128)(2,1)}) %all-gather.4.cloned.1.call-update) | async-done | bytes 10485776 | tf_op jit(solution)/shard_map/all_gather | solution.py:162
  195.2 8.6 fusion.69
  203.8 18.4 %fusion.70 = f32[1024,5120]{1,0:T(8,128)} fusion(bf16[256,5120]{0,1:T(8,128)(2,1)} %bitcast.76, bf16[1024,5120]{1,0:T(8,128)(2,1)} %all-gather.4.cloned.1.call-done, bf16[5120,256]{1,0:T(8,128)(2,1)S(1)} %copy-done, f32[1024,256]{1,0:T(8,128)} %fusion.69), kind=kOutput, calls=%fused_computation.86 | convolution fusion | flops 5370281984 | bytes 37748736 | tf_op jit(solution)/shard_map/dot_general | solution.py:178
  222.3 674.4 %reduce-scatter.2.cloned.1.call-done = f32[8,5120]{1,0:T(8,128)} async-done(((f32[1024,5120]{1,0:T(8,128)}), f32[8,5120]{1,0:T(8,128)}) %reduce-scatter.2.cloned.1.call-update) | async-done | bytes 163856 | tf_op jit(solution)/shard_map/reduce_scatter | solution.py:177
  (88 shorter events, 30.1 us)
Async XLA Ops:
  6.5 197.3 %copy-start = (bf16[5120,256]{1,0:T(8,128)(2,1)S(1)}, bf16[5120,256]{1,0:T(8,128)(2,1)}, u32[]{:S(2)}) copy-start(bf16[5120,256]{1,0:T(8,128)(2,1)} %param.32) | copy-start | bytes 7864324
  6.5 17.4 %copy-start.8 = (bf16[32,256]{1,0:T(8,128)(2,1)S(1)}, bf16[32,256]{1,0:T(8,128)(2,1)}, u32[]{:S(2)}) copy-start(bf16[32,256]{1,0:T(8,128)(2,1)} %param.20) | copy-start | bytes 49156
  9.0 20.1 %all-to-all-start = ((s32[32,1,2]{2,1,0:T(1,128)}), s32[32,1,2]{2,1,0:T(1,128)S(1)}, u32[]{:S(2)}, u32[]{:S(2)}) async-start(s32[32,1,2]{2,1,0:T(1,128)} %bitcast), calls=%async_computation | async-start | bytes 32768 | tf_op jit(solution)/shard_map/all_to_all | solution.py:67
  23.8 2.6 copy-start.4
  29.2 15.3 %all-to-all-start.1 = ((bf16[32,2,1024]{2,1,0:T(2,128)(2,1)}), bf16[32,2,1024]{2,1,0:T(2,128)(2,1)}, u32[]{:S(2)}, u32[]{:S(2)}) async-start(bf16[32,2,1024]{2,1,0:T(2,128)(2,1)} %reshape.200), calls=%async_computation.1 | async-start | bytes 262144 | tf_op jit(solution)/shard_map/all_to_all | solution.py:66
  47.8 1.7 copy-start.2
  47.8 7.0 copy-start.11
  47.8 7.6 copy-start.6
  47.9 9.7 %copy-start.10 = (bf16[32,2,4]{0,2,1:T(4,128)(2,1)S(1)}, bf16[32,2,4]{0,2,1:T(4,128)(2,1)}, u32[]{:S(2)}) copy-start(bf16[32,2,4]{0,2,1:T(4,128)(2,1)} %get-tuple-element.8) | copy-start | bytes 1540
  47.9 10.4 %copy-start.9 = (bf16[32,256]{1,0:T(8,128)(2,1)S(1)}, bf16[32,256]{1,0:T(8,128)(2,1)}, u32[]{:S(2)}) copy-start(bf16[32,256]{1,0:T(8,128)(2,1)} %param.21) | copy-start | bytes 49156
  51.0 11.3 %all-to-all-start.4 = ((f32[32,2,8]{2,1,0:T(2,128)}), f32[32,2,8]{2,1,0:T(2,128)S(1)}, u32[]{:S(2)}, u32[]{:S(2)}) async-start(f32[32,2,8]{2,1,0:T(2,128)} %reshape.213), calls=%async_computation.4 | async-start | bytes 65536 | tf_op jit(solution)/shard_map/all_to_all | solution.py:101
  62.2 12.3 %all-to-all-start.3 = ((f32[32,2,8]{2,1,0:T(2,128)}), f32[32,2,8]{2,1,0:T(2,128)S(1)}, u32[]{:S(2)}, u32[]{:S(2)}) async-start(f32[32,2,8]{2,1,0:T(2,128)} %reshape.206), calls=%async_computation.3 | async-start | bytes 65536 | tf_op jit(solution)/shard_map/all_to_all | solution.py:94
  69.8 19.1 %copy-start.5 = (f32[32,2,4,160]{3,2,1,0:T(4,128)S(1)}, f32[32,2,4,160]{3,2,1,0:T(4,128)}, u32[]{:S(2)}) copy-start(f32[32,2,4,160]{3,2,1,0:T(4,128)} %copy-done.4) | copy-start | bytes 491524
  74.6 13.3 %all-to-all-start.2 = ((f32[32,2,1024]{2,1,0:T(2,128)}), f32[32,2,1024]{2,1,0:T(2,128)S(1)}, u32[]{:S(2)}, u32[]{:S(2)}) async-start(f32[32,2,1024]{2,1,0:T(2,128)} %reshape.204), calls=%async_computation.2 | async-start | bytes 524288 | tf_op jit(solution)/shard_map/all_to_all | solution.py:87
  78.9 53.7 %all-gather.6.cloned.1.call-start = ((), (), s32[]{:S(2)}) async-start(), calls=%async_computation.9 | async-start | bytes 3276800 | tf_op jit(solution)/shard_map/all_gather | solution.py:159
  98.3 38.3 %copy-start.7 = (f32[5120]{0:T(1024)S(1)}, f32[5120]{0:T(1024)}, u32[]{:S(2)}) copy-start(f32[5120]{0:T(1024)} %param.30) | copy-start | bytes 61444
  98.3 97.0 %all-gather.4.cloned.1.call-start = ((), (), s32[]{:S(2)}) async-start(), calls=%async_computation.7 | async-start | bytes 10813440 | tf_op jit(solution)/shard_map/all_gather | solution.py:162
  135.8 0.7 copy-start.3
  137.4 759.2 %reduce-scatter.2.cloned.1.call-start = ((), (), s32[]{:S(2)}) async-start(), calls=%async_computation.8 | async-start | bytes 21135360 | tf_op jit(solution)/shard_map/reduce_scatter | solution.py:177
  222.3 676.0 %copy-start.1 = (bf16[5120,256]{1,0:T(8,128)(2,1)S(1)}, bf16[5120,256]{1,0:T(8,128)(2,1)}, u32[]{:S(2)}) copy-start(bf16[5120,256]{1,0:T(8,128)(2,1)} %param.32) | copy-start | bytes 7864324
Sparse Core Ops, SparseCore 0:
  98.4 34.2 all-gather.5
  137.5 57.6 all-gather.3
  222.4 674.2 reduce-scatter.1
